TPU v7x, 32 devices: a whole 2x2x4 slice. The times are simulated.
32 devices in a mesh: row: 8 (over z, x), col: 4 (over y, core).
Axes of the slice: x: 2, y: 2, z: 4, core: 2. Of those that a mesh axis runs over, the one named last changes fastest.
Arguments:
- src_points: bfloat16 [64, 8192], P(None, ('row', 'col')), may hold values from -24 to 24
- tgt_points: bfloat16 [64, 4096], P(None, ('col', 'row')), may hold values from -24 to 24
- grad_f: float32 [8192], P('row'), may hold values from -6 to 6
- grad_g: float32 [4096], P('col'), may hold values from -6 to 6
Outputs:
- grad_src: float32 [64, 8192], P(None, ('row', 'col'))
- grad_tgt: float32 [64, 4096], P(None, ('col', 'row'))
All inputs are finite; a program needn't handle non-finite values.
Results may differ from a plain program's by a relative error of at most 0.0085.
Values may be sent and summed in bfloat16 or wider, within the bound.
No kernel may reach another device: no remote copies, remote signals or barrier semaphores. Data moves between devices by JAX's collectives and lax.ppermute only.
A program may use at most 64 MiB of HBM per device.

v0:
```python
import math
import jax
import jax.numpy as jnp
from jax import lax
from jax.sharding import PartitionSpec as P

SINK = 2
CG = 3
EPS = 4.0
TAU = 0.1


def cost_tile(block_pts, block_sq, points_col, sq_col):
    cross = lax.dot_general(
        block_pts, points_col, (((0,), (0,)), ((), ())), preferred_element_type=jnp.float32
    )
    return block_sq[:, None] + sq_col[None, :] - 2.0 * cross


def body(src_points, tgt_points, grad_f, grad_g):
    points_row = lax.all_gather(src_points, "col", axis=1, tiled=True)
    points_col = lax.all_gather(tgt_points, "row", axis=1, tiled=True)
    sq_row = jnp.sum(jnp.square(points_row.astype(jnp.float32)), axis=0)
    sq_col = jnp.sum(jnp.square(points_col.astype(jnp.float32)), axis=0)
    features, row_count = points_row.shape
    col_count = points_col.shape[1]
    block = min(512, row_count)
    block_count = row_count // block
    blocks_pts = jnp.moveaxis(points_row.reshape(features, block_count, block), 1, 0)
    blocks_sq = sq_row.reshape(block_count, block)
    shift = EPS * math.log(lax.axis_size("row") / lax.axis_size("col"))
    pot_col = jnp.zeros((col_count,), jnp.float32)
    pot_row = jnp.zeros((row_count,), jnp.float32)
    for iteration in range(SINK):

        def row_scores(block_pts, block_sq):
            return (pot_col[None, :] - cost_tile(block_pts, block_sq, points_col, sq_col)) / EPS

        def maxima(pieces):
            return jnp.max(row_scores(pieces[0], pieces[1]), axis=1)

        row_highest = lax.pmax(lax.map(maxima, (blocks_pts, blocks_sq)).reshape(-1), "col")

        def sums(pieces):
            return jnp.sum(jnp.exp(row_scores(pieces[0], pieces[1]) - pieces[2][:, None]), axis=1)

        local = lax.map(
            sums, (blocks_pts, blocks_sq, row_highest.reshape(block_count, block))
        ).reshape(-1)
        row_totals = lax.psum(local, "col")
        pot_row = -EPS * (row_highest + jnp.log(row_totals))
        blocks_pot = pot_row.reshape(block_count, block)

        def scores(pieces):
            return (pieces[2][:, None] - cost_tile(pieces[0], pieces[1], points_col, sq_col)) / EPS

        lowest = jnp.full((col_count,), -jnp.inf, jnp.float32)
        empty = jnp.zeros((col_count,), jnp.float32)

        def max_step(carry, pieces):
            return (jnp.maximum(carry, jnp.max(scores(pieces), axis=0)), None)

        highest, unused = lax.scan(max_step, lowest, (blocks_pts, blocks_sq, blocks_pot))
        highest = lax.pmax(highest, "row")

        def sum_step(carry, pieces):
            return (carry + jnp.sum(jnp.exp(scores(pieces) - highest[None, :]), axis=0), None)

        totals, unused = lax.scan(sum_step, empty, (blocks_pts, blocks_sq, blocks_pot))
        totals = lax.psum(totals, "row")
        pot_col = shift - EPS * (highest + jnp.log(totals))

    def plan_rows(pieces):
        cost = cost_tile(pieces[0], pieces[1], points_col, sq_col)
        return jnp.exp((pieces[2][:, None] + pot_col[None, :] - cost) / EPS).astype(jnp.bfloat16)

    plan_tile = lax.map(
        plan_rows, (blocks_pts, blocks_sq, pot_row.reshape(block_count, block))
    ).reshape(row_count, col_count)

    def row_dot(vector):
        return jnp.sum(plan_tile * vector[None, :], axis=1)

    def col_dot(vector):
        return jnp.sum(plan_tile * vector[:, None], axis=0)

    row_mass = lax.psum(jnp.sum(plan_tile, axis=1, dtype=jnp.float32), "col")
    col_mass, pulled = lax.psum(
        (jnp.sum(plan_tile, axis=0, dtype=jnp.float32), col_dot(grad_f / row_mass)), "row"
    )
    rhs = grad_g - pulled

    def norm_sum(vector):
        return lax.psum(jnp.sum(vector * vector), "col")

    dual_col = jnp.zeros_like(rhs)
    residual = rhs
    direction = rhs
    norm_now = norm_sum(residual)
    for iteration in range(CG):
        applied = lax.psum(row_dot(direction), "col")
        back = lax.psum(col_dot(applied / row_mass), "row")
        image = (1.0 + TAU) * col_mass * direction - back
        alpha = norm_now / lax.psum(jnp.sum(direction * image), "col")
        dual_col = dual_col + alpha * direction
        residual = residual - alpha * image
        norm_next = norm_sum(residual)
        direction = residual + norm_next / norm_now * direction
        norm_now = norm_next
    dual_row = (grad_f - lax.psum(row_dot(dual_col), "col")) / row_mass
    weights = (plan_tile * (dual_row[:, None] + dual_col[None, :])).astype(jnp.bfloat16)
    rows_w = jnp.sum(weights, axis=1, dtype=jnp.float32)
    cols_w = jnp.sum(weights, axis=0, dtype=jnp.float32)
    pulled_src = lax.dot_general(
        points_col, weights, (((1,), (1,)), ((), ())), preferred_element_type=jnp.float32
    )
    pulled_tgt = lax.dot_general(
        points_row, weights, (((1,), (0,)), ((), ())), preferred_element_type=jnp.float32
    )
    part_src = 2.0 * (points_row.astype(jnp.float32) * rows_w[None, :] - pulled_src)
    part_tgt = 2.0 * (points_col.astype(jnp.float32) * cols_w[None, :] - pulled_tgt)
    grad_src = lax.psum_scatter(part_src, "col", scatter_dimension=1, tiled=True)
    grad_tgt = lax.psum_scatter(part_tgt, "row", scatter_dimension=1, tiled=True)
    return (grad_src, grad_tgt)


def solution(mesh):
    in_specs = (P(None, ("row", "col")), P(None, ("col", "row")), P("row"), P("col"))
    out_specs = (P(None, ("row", "col")), P(None, ("col", "row")))
    return jax.shard_map(body, mesh=mesh, in_specs=in_specs, out_specs=out_specs, check_vma=False)
```

profile of v0, /device:TPU:0, one launch (start us, length us, event | category | flops | bytes accessed | tf_op | source)
XLA Modules:
  0.0 396.4 jit_solution(7634466997313843352)
XLA Ops:
  7.3 28.2 %all_gather.7 = bf16[64,1024]{1,0:T(8,128)(2,1)S(1)} all-gather(bf16[64,128]{1,0:T(8,128)(2,1)} %param.23), channel_id=1, replica_groups=mesh['row'=8,'col'=4] {'row'}, dimensions={1}, use_global_device_ids=true | all-gather | bytes 147456 | tf_op jit(solution)/shard_map/all_gather | solution.py:22
  42.7 7.1 %pmax.28 = f32[1024]{0:T(1024)S(1)} all-reduce(f32[1024]{0:T(1024)S(1)} %bitcast.218), channel_id=1, replica_groups=mesh['row'=8,'col'=4] {'col'}, use_global_device_ids=true, to_apply=%region_5.6 | all-reduce | flops 1024 | bytes 8192 | tf_op jit(solution)/shard_map/pmax | solution.py:42
  51.8 5.9 %psum.140 = f32[1024]{0:T(1024)S(1)} all-reduce(f32[1024]{0:T(1024)S(1)} %bitcast.219), channel_id=1, replica_groups=mesh['row'=8,'col'=4] {'col'}, use_global_device_ids=true, to_apply=%region_9.10 | all-reduce | flops 1024 | bytes 8192 | tf_op jit(solution)/shard_map/psum | solution.py:50
  59.1 19.7 %pmax.29 = f32[1024]{0:T(1024)S(1)} all-reduce(f32[1024]{0:T(1024)S(1)} %get-tuple-element.352), channel_id=1, replica_groups=mesh['row'=8,'col'=4] {'row'}, use_global_device_ids=true, to_apply=%region_13.14 | all-reduce | flops 1024 | bytes 8192 | tf_op jit(solution)/shard_map/pmax | solution.py:64
  80.5 17.1 %psum.141 = f32[1024]{0:T(1024)S(1)} all-reduce(f32[1024]{0:T(1024)S(1)} %get-tuple-element.353), channel_id=1, replica_groups=mesh['row'=8,'col'=4] {'row'}, use_global_device_ids=true, to_apply=%region_17.18 | all-reduce | flops 1024 | bytes 8192 | tf_op jit(solution)/shard_map/psum | solution.py:70
  99.2 5.8 %pmax.30 = f32[1024]{0:T(1024)S(1)} all-reduce(f32[1024]{0:T(1024)S(1)} %bitcast.220), channel_id=1, replica_groups=mesh['row'=8,'col'=4] {'col'}, use_global_device_ids=true, to_apply=%region_21.22 | all-reduce | flops 1024 | bytes 8192 | tf_op jit(solution)/shard_map/pmax | solution.py:42
  107.0 5.8 %psum.142 = f32[1024]{0:T(1024)S(1)} all-reduce(f32[1024]{0:T(1024)S(1)} %bitcast.221), channel_id=1, replica_groups=mesh['row'=8,'col'=4] {'col'}, use_global_device_ids=true, to_apply=%region_25.26 | all-reduce | flops 1024 | bytes 8192 | tf_op jit(solution)/shard_map/psum | solution.py:50
  114.1 19.1 %pmax.31 = f32[1024]{0:T(1024)S(1)} all-reduce(f32[1024]{0:T(1024)S(1)} %get-tuple-element.356), channel_id=1, replica_groups=mesh['row'=8,'col'=4] {'row'}, use_global_device_ids=true, to_apply=%region_29.30 | all-reduce | flops 1024 | bytes 8192 | tf_op jit(solution)/shard_map/pmax | solution.py:64
  135.0 17.1 %psum.143 = f32[1024]{0:T(1024)S(1)} all-reduce(f32[1024]{0:T(1024)S(1)} %get-tuple-element.357), channel_id=1, replica_groups=mesh['row'=8,'col'=4] {'row'}, use_global_device_ids=true, to_apply=%region_33.34 | all-reduce | flops 1024 | bytes 8192 | tf_op jit(solution)/shard_map/psum | solution.py:70
  161.0 19.1 %psum.145 = f32[1024]{0:T(1024)S(1)} all-reduce(f32[1024]{0:T(1024)S(1)} %fusion.29), channel_id=1, replica_groups=mesh['row'=8,'col'=4] {'row'}, use_global_device_ids=true, to_apply=%region_39.40 | all-reduce | flops 1024 | bytes 8192 | tf_op jit(solution)/shard_map/psum | solution.py:88
  180.6 5.7 %psum.148 = f32[1024]{0:T(1024)S(1)} all-reduce(f32[1024]{0:T(1024)S(1)} %bitcast.223), channel_id=1, replica_groups=mesh['row'=8,'col'=4] {'col'}, use_global_device_ids=true, to_apply=%region_45.46 | all-reduce | flops 1024 | bytes 8192 | tf_op jit(solution)/shard_map/psum | solution.py:101
  186.8 17.4 %all-reduce = (f32[1024]{0:T(1024)S(1)}, f32[1024]{0:T(1024)S(1)}) all-reduce(f32[1024]{0:T(1024)S(1)} %fusion.31, f32[1024]{0:T(1024)S(1)} %get-tuple-element.463), channel_id=1, replica_groups=mesh['row'=8,'col'=4] {'row'}, use_global_device_ids=true, to_apply=%region_47.48 | all-reduce | flops 2048 | bytes 16384 | tf_op jit(solution)/shard_map/psum | solution.py:102
  204.8 6.3 %all-reduce.1 = (f32[]{:T(128)}, f32[]{:T(128)}) all-reduce(f32[]{:T(128)} %get-tuple-element.466, f32[]{:T(128)} %get-tuple-element.465), channel_id=1, replica_groups=mesh['row'=8,'col'=4] {'col'}, use_global_device_ids=true, to_apply=%region_41.42 | all-reduce | flops 2 | bytes 16 | tf_op jit(solution)/shard_map/psum | solution.py:94
  213.0 7.5 %psum.151 = f32[]{:T(128)} all-reduce(f32[]{:T(128)} %get-tuple-element.605), channel_id=1, replica_groups=mesh['row'=8,'col'=4] {'col'}, use_global_device_ids=true, to_apply=%region_51.52 | all-reduce | flops 1 | bytes 8 | tf_op jit(solution)/shard_map/psum | solution.py:94
  222.4 5.7 %psum.152 = f32[1024]{0:T(1024)S(1)} all-reduce(f32[1024]{0:T(1024)S(1)} %bitcast.224), channel_id=1, replica_groups=mesh['row'=8,'col'=4] {'col'}, use_global_device_ids=true, to_apply=%region_53.54 | all-reduce | flops 1024 | bytes 8192 | tf_op jit(solution)/shard_map/psum | solution.py:101
  228.5 19.2 %psum.153 = f32[1024]{0:T(1024)S(1)} all-reduce(f32[1024]{0:T(1024)S(1)} %fusion.33), channel_id=1, replica_groups=mesh['row'=8,'col'=4] {'row'}, use_global_device_ids=true, to_apply=%region_55.56 | all-reduce | flops 1024 | bytes 8192 | tf_op jit(solution)/shard_map/psum | solution.py:102
  248.3 6.3 %psum.154 = f32[]{:T(128)} all-reduce(f32[]{:T(128)} %multiply_reduce_fusion.6), channel_id=1, replica_groups=mesh['row'=8,'col'=4] {'col'}, use_global_device_ids=true, to_apply=%region_57.58 | all-reduce | flops 1 | bytes 8 | tf_op jit(solution)/shard_map/psum | solution.py:104
  256.5 6.7 %psum.155 = f32[]{:T(128)} all-reduce(f32[]{:T(128)} %get-tuple-element.603), channel_id=1, replica_groups=mesh['row'=8,'col'=4] {'col'}, use_global_device_ids=true, to_apply=%region_59.60 | all-reduce | flops 1 | bytes 8 | tf_op jit(solution)/shard_map/psum | solution.py:94
  265.0 5.7 %psum.156 = f32[1024]{0:T(1024)S(1)} all-reduce(f32[1024]{0:T(1024)S(1)} %bitcast.225), channel_id=1, replica_groups=mesh['row'=8,'col'=4] {'col'}, use_global_device_ids=true, to_apply=%region_61.62 | all-reduce | flops 1024 | bytes 8192 | tf_op jit(solution)/shard_map/psum | solution.py:101
  271.2 17.1 %psum.157 = f32[1024]{0:T(1024)S(1)} all-reduce(f32[1024]{0:T(1024)S(1)} %fusion.35), channel_id=1, replica_groups=mesh['row'=8,'col'=4] {'row'}, use_global_device_ids=true, to_apply=%region_63.64 | all-reduce | flops 1024 | bytes 8192 | tf_op jit(solution)/shard_map/psum | solution.py:102
  289.0 6.3 %psum.158 = f32[]{:T(128)} all-reduce(f32[]{:T(128)} %multiply_reduce_fusion.4), channel_id=1, replica_groups=mesh['row'=8,'col'=4] {'col'}, use_global_device_ids=true, to_apply=%region_65.66 | all-reduce | flops 1 | bytes 8 | tf_op jit(solution)/shard_map/psum | solution.py:104
  297.1 6.7 %psum.159 = f32[1024]{0:T(1024)S(1)} all-reduce(f32[1024]{0:T(1024)S(1)} %bitcast.226), channel_id=1, replica_groups=mesh['row'=8,'col'=4] {'col'}, use_global_device_ids=true, to_apply=%region_67.68 | all-reduce | flops 1024 | bytes 8192 | tf_op jit(solution)/shard_map/psum | solution.py:110
  310.1 57.3 %reduce-scatter.5.cloned.1.call-done = f32[64,128]{1,0:T(8,128)} async-done(((f32[64,1024]{1,0:T(8,128)}), f32[64,128]{1,0:T(8,128)}) %reduce-scatter.5.cloned.1.call-update) | async-done | bytes 32784 | tf_op jit(solution)/shard_map/reduce_scatter | solution.py:123
  367.5 22.1 %reduce-scatter.3.cloned.1.call-done = f32[64,256]{1,0:T(8,128)} async-done(((f32[64,1024]{1,0:T(8,128)}), f32[64,256]{1,0:T(8,128)}) %reduce-scatter.3.cloned.1.call-update) | async-done | bytes 65552 | tf_op jit(solution)/shard_map/reduce_scatter | solution.py:122
  (136 shorter events, 54.9 us)
Async XLA Ops:
  7.2 360.3 %reduce-scatter.5.cloned.1.call-start = ((), (), s32[]{:S(2)}) async-start(), calls=%async_computation.3 | async-start | bytes 294912 | tf_op jit(solution)/shard_map/reduce_scatter | solution.py:123
  153.9 6.6 %copy-start.1 = (f32[1024]{0:T(1024)S(1)}, f32[1024]{0:T(1024)}, u32[]{:S(2)}) copy-start(f32[1024]{0:T(1024)} %param.24) | copy-start | bytes 12292
  153.9 26.2 %copy-start.2 = (f32[1024]{0:T(1024)S(1)}, f32[1024]{0:T(1024)}, u32[]{:S(2)}) copy-start(f32[1024]{0:T(1024)} %param.25) | copy-start | bytes 12292
  304.4 1.4 copy-start
  306.9 82.7 %reduce-scatter.3.cloned.1.call-start = ((), (), s32[]{:S(2)}) async-start(), calls=%async_computation.2 | async-start | bytes 327680 | tf_op jit(solution)/shard_map/reduce_scatter | solution.py:122
Sparse Core Ops, SparseCore 0:
  307.1 60.3 reduce-scatter.4
  370.5 19.0 reduce-scatter.2
where the time goes:
time: 397 us; the launch traced here: 396 us
  blocking collectives  267 us (67%)
  waiting for transfers between devices  79.5 us (20%)
  between operations  21 us (5%)
  matrix products  18.1 us (5%)
  other arithmetic  9.57 us (2%)
    reduce_scatter x1, waiting for transfers between devices, body(): lax.psum_scatter(part_tgt, 'row', scatter_dimension=1, tiled=True)  57.3 us
    psum x3, blocking collectives, body(): back = lax.psum(col_dot(applied / row_mass), 'row')  53.7 us
    pmax x2, blocking collectives, body(): highest = lax.pmax(highest, 'row')  38.8 us
    psum x2, blocking collectives, body(): totals = lax.psum(totals, 'row')  34.3 us
    all_gather x1, blocking collectives, body(): points_col = lax.all_gather(tgt_points, 'row', axis=1, tiled=True)  28.2 us
    reduce_scatter x1, waiting for transfers between devices, body(): lax.psum_scatter(part_src, 'col', scatter_dimension=1, tiled=True)  22.1 us
    psum x3, blocking collectives, norm_sum(): return lax.psum(jnp.sum(vector * vector), 'col')  20.4 us
    psum x1, blocking collectives, body(): lax.psum((jnp.sum(plan_tile, axis=0, dtype=jnp.float32), col_dot(grad_f /...  19.1 us
  transfers between devices with their start and end apart: 2, of which 2 were waited for; matrix products, arithmetic and copies ran while one was open for 1% of the time, Pallas kernels for 0%

commit v1 on v0

--- a/solution.py
+++ b/solution.py
@@ -99,7 +99,9 @@
     norm_now = norm_sum(residual)
     for iteration in range(CG):
         applied = lax.psum(row_dot(direction), "col")
-        back = lax.psum(col_dot(applied / row_mass), "row")
+        own = col_dot(applied / row_mass)
+        parts = lax.all_gather(own, "row", axis=0, tiled=False)
+        back = parts.sum(axis=0)
         image = (1.0 + TAU) * col_mass * direction - back
         alpha = norm_now / lax.psum(jnp.sum(direction * image), "col")
         dual_col = dual_col + alpha * direction

time: 397 us -> 434 us (1.093)
  blocking collectives: 267 us -> 305 us
    all_gather x0 -> x3, blocking collectives: none -> 91.8 us  [body(): parts = lax.all_gather(own, 'row', axis=0, tiled=False)]
    psum x3 -> x0, blocking collectives: 53.7 us -> none  [body(): back = lax.psum(col_dot(applied / row_mass), 'row')]
where the time goes in v1:
time: 434 us; the launch traced here: 433 us
  blocking collectives  305 us (70%)
  waiting for transfers between devices  78.1 us (18%)
  between operations  21.1 us (5%)
  matrix products  18.1 us (4%)
  other arithmetic  9.61 us (2%)
    all_gather x3, blocking collectives, body(): parts = lax.all_gather(own, 'row', axis=0, tiled=False)  91.8 us
    reduce_scatter x1, waiting for transfers between devices, body(): lax.psum_scatter(part_tgt, 'row', scatter_dimension=1, tiled=True)  55.8 us
    pmax x2, blocking collectives, body(): highest = lax.pmax(highest, 'row')  38.8 us
    psum x2, blocking collectives, body(): totals = lax.psum(totals, 'row')  34.3 us
    all_gather x1, blocking collectives, body(): points_col = lax.all_gather(tgt_points, 'row', axis=1, tiled=True)  28.2 us
    reduce_scatter x1, waiting for transfers between devices, body(): lax.psum_scatter(part_src, 'col', scatter_dimension=1, tiled=True)  22.2 us
    psum x3, blocking collectives, norm_sum(): return lax.psum(jnp.sum(vector * vector), 'col')  20.4 us
    psum x1, blocking collectives, body(): lax.psum((jnp.sum(plan_tile, axis=0, dtype=jnp.float32), col_dot(grad_f /...  19.4 us
  transfers between devices with their start and end apart: 2, of which 2 were waited for; matrix products, arithmetic and copies ran while one was open for 1% of the time, Pallas kernels for 0%

profile of v1, /device:TPU:0, one launch (start us, length us, event | category | flops | bytes accessed | tf_op | source)
XLA Modules:
  0.0 433.5 jit_solution(11187604535859390233)
XLA Ops:
  7.3 28.2 %all_gather.25 = bf16[64,1024]{1,0:T(8,128)(2,1)S(1)} all-gather(bf16[64,128]{1,0:T(8,128)(2,1)} %param.23), channel_id=1, replica_groups=mesh['row'=8,'col'=4] {'row'}, dimensions={1}, use_global_device_ids=true | all-gather | bytes 147456 | tf_op jit(solution)/shard_map/all_gather | solution.py:22
  42.7 7.1 %pmax.28 = f32[1024]{0:T(1024)S(1)} all-reduce(f32[1024]{0:T(1024)S(1)} %bitcast.218), channel_id=1, replica_groups=mesh['row'=8,'col'=4] {'col'}, use_global_device_ids=true, to_apply=%region_5.6 | all-reduce | flops 1024 | bytes 8192 | tf_op jit(solution)/shard_map/pmax | solution.py:42
  51.8 5.9 %psum.119 = f32[1024]{0:T(1024)S(1)} all-reduce(f32[1024]{0:T(1024)S(1)} %bitcast.219), channel_id=1, replica_groups=mesh['row'=8,'col'=4] {'col'}, use_global_device_ids=true, to_apply=%region_9.10 | all-reduce | flops 1024 | bytes 8192 | tf_op jit(solution)/shard_map/psum | solution.py:50
  59.1 19.7 %pmax.29 = f32[1024]{0:T(1024)S(1)} all-reduce(f32[1024]{0:T(1024)S(1)} %get-tuple-element.352), channel_id=1, replica_groups=mesh['row'=8,'col'=4] {'row'}, use_global_device_ids=true, to_apply=%region_13.14 | all-reduce | flops 1024 | bytes 8192 | tf_op jit(solution)/shard_map/pmax | solution.py:64
  80.5 17.1 %psum.120 = f32[1024]{0:T(1024)S(1)} all-reduce(f32[1024]{0:T(1024)S(1)} %get-tuple-element.353), channel_id=1, replica_groups=mesh['row'=8,'col'=4] {'row'}, use_global_device_ids=true, to_apply=%region_17.18 | all-reduce | flops 1024 | bytes 8192 | tf_op jit(solution)/shard_map/psum | solution.py:70
  99.2 5.8 %pmax.30 = f32[1024]{0:T(1024)S(1)} all-reduce(f32[1024]{0:T(1024)S(1)} %bitcast.220), channel_id=1, replica_groups=mesh['row'=8,'col'=4] {'col'}, use_global_device_ids=true, to_apply=%region_21.22 | all-reduce | flops 1024 | bytes 8192 | tf_op jit(solution)/shard_map/pmax | solution.py:42
  107.0 5.8 %psum.121 = f32[1024]{0:T(1024)S(1)} all-reduce(f32[1024]{0:T(1024)S(1)} %bitcast.221), channel_id=1, replica_groups=mesh['row'=8,'col'=4] {'col'}, use_global_device_ids=true, to_apply=%region_25.26 | all-reduce | flops 1024 | bytes 8192 | tf_op jit(solution)/shard_map/psum | solution.py:50
  114.1 19.1 %pmax.31 = f32[1024]{0:T(1024)S(1)} all-reduce(f32[1024]{0:T(1024)S(1)} %get-tuple-element.356), channel_id=1, replica_groups=mesh['row'=8,'col'=4] {'row'}, use_global_device_ids=true, to_apply=%region_29.30 | all-reduce | flops 1024 | bytes 8192 | tf_op jit(solution)/shard_map/pmax | solution.py:64
  135.0 17.1 %psum.122 = f32[1024]{0:T(1024)S(1)} all-reduce(f32[1024]{0:T(1024)S(1)} %get-tuple-element.357), channel_id=1, replica_groups=mesh['row'=8,'col'=4] {'row'}, use_global_device_ids=true, to_apply=%region_33.34 | all-reduce | flops 1024 | bytes 8192 | tf_op jit(solution)/shard_map/psum | solution.py:70
  161.0 19.4 %all-reduce = (f32[1024]{0:T(1024)S(1)}, f32[1024]{0:T(1024)S(1)}) all-reduce(f32[1024]{0:T(1024)S(1)} %fusion.29, f32[1024]{0:T(1024)S(1)} %get-tuple-element.463), channel_id=1, replica_groups=mesh['row'=8,'col'=4] {'row'}, use_global_device_ids=true, to_apply=%region_39.40 | all-reduce | flops 2048 | bytes 16384 | tf_op jit(solution)/shard_map/psum | solution.py:88
  180.9 5.7 %psum.127 = f32[1024]{0:T(1024)S(1)} all-reduce(f32[1024]{0:T(1024)S(1)} %bitcast.223), channel_id=1, replica_groups=mesh['row'=8,'col'=4] {'col'}, use_global_device_ids=true, to_apply=%region_45.46 | all-reduce | flops 1024 | bytes 8192 | tf_op jit(solution)/shard_map/psum | solution.py:101
  187.1 30.6 %all-gather = f32[8192]{0:T(1024)S(1)} all-gather(f32[1024]{0:T(1024)S(1)} %fusion.31), channel_id=2, replica_groups=mesh['row'=8,'col'=4] {'row'}, dimensions={0}, use_global_device_ids=true | all-gather | bytes 36864 | tf_op jit(solution)/shard_map/all_gather | solution.py:103
  218.3 6.3 %all-reduce.1 = (f32[]{:T(128)}, f32[]{:T(128)}) all-reduce(f32[]{:T(128)} %get-tuple-element.466, f32[]{:T(128)} %get-tuple-element.465), channel_id=1, replica_groups=mesh['row'=8,'col'=4] {'col'}, use_global_device_ids=true, to_apply=%region_41.42 | all-reduce | flops 2 | bytes 16 | tf_op jit(solution)/shard_map/psum | solution.py:94
  226.5 7.5 %psum.129 = f32[]{:T(128)} all-reduce(f32[]{:T(128)} %get-tuple-element.605), channel_id=1, replica_groups=mesh['row'=8,'col'=4] {'col'}, use_global_device_ids=true, to_apply=%region_51.52 | all-reduce | flops 1 | bytes 8 | tf_op jit(solution)/shard_map/psum | solution.py:94
  235.9 5.7 %psum.130 = f32[1024]{0:T(1024)S(1)} all-reduce(f32[1024]{0:T(1024)S(1)} %bitcast.224), channel_id=1, replica_groups=mesh['row'=8,'col'=4] {'col'}, use_global_device_ids=true, to_apply=%region_53.54 | all-reduce | flops 1024 | bytes 8192 | tf_op jit(solution)/shard_map/psum | solution.py:101
  242.0 30.6 %all-gather.1 = f32[8192]{0:T(1024)S(1)} all-gather(f32[1024]{0:T(1024)S(1)} %fusion.33), channel_id=3, replica_groups=mesh['row'=8,'col'=4] {'row'}, dimensions={0}, use_global_device_ids=true | all-gather | bytes 36864 | tf_op jit(solution)/shard_map/all_gather | solution.py:103
  273.3 6.3 %psum.131 = f32[]{:T(128)} all-reduce(f32[]{:T(128)} %multiply_reduce_fusion.6), channel_id=1, replica_groups=mesh['row'=8,'col'=4] {'col'}, use_global_device_ids=true, to_apply=%region_57.58 | all-reduce | flops 1 | bytes 8 | tf_op jit(solution)/shard_map/psum | solution.py:106
  281.5 6.7 %psum.132 = f32[]{:T(128)} all-reduce(f32[]{:T(128)} %get-tuple-element.603), channel_id=1, replica_groups=mesh['row'=8,'col'=4] {'col'}, use_global_device_ids=true, to_apply=%region_59.60 | all-reduce | flops 1 | bytes 8 | tf_op jit(solution)/shard_map/psum | solution.py:94
  290.0 5.7 %psum.133 = f32[1024]{0:T(1024)S(1)} all-reduce(f32[1024]{0:T(1024)S(1)} %bitcast.225), channel_id=1, replica_groups=mesh['row'=8,'col'=4] {'col'}, use_global_device_ids=true, to_apply=%region_61.62 | all-reduce | flops 1024 | bytes 8192 | tf_op jit(solution)/shard_map/psum | solution.py:101
  296.2 30.6 %all-gather.2 = f32[8192]{0:T(1024)S(1)} all-gather(f32[1024]{0:T(1024)S(1)} %fusion.35), channel_id=4, replica_groups=mesh['row'=8,'col'=4] {'row'}, dimensions={0}, use_global_device_ids=true | all-gather | bytes 36864 | tf_op jit(solution)/shard_map/all_gather | solution.py:103
  327.5 6.3 %psum.134 = f32[]{:T(128)} all-reduce(f32[]{:T(128)} %multiply_reduce_fusion.4), channel_id=1, replica_groups=mesh['row'=8,'col'=4] {'col'}, use_global_device_ids=true, to_apply=%region_65.66 | all-reduce | flops 1 | bytes 8 | tf_op jit(solution)/shard_map/psum | solution.py:106
  335.6 6.7 %psum.135 = f32[1024]{0:T(1024)S(1)} all-reduce(f32[1024]{0:T(1024)S(1)} %bitcast.226), channel_id=1, replica_groups=mesh['row'=8,'col'=4] {'col'}, use_global_device_ids=true, to_apply=%region_67.68 | all-reduce | flops 1024 | bytes 8192 | tf_op jit(solution)/shard_map/psum | solution.py:112
  348.6 55.8 %reduce-scatter.5.cloned.1.call-done = f32[64,128]{1,0:T(8,128)} async-done(((f32[64,1024]{1,0:T(8,128)}), f32[64,128]{1,0:T(8,128)}) %reduce-scatter.5.cloned.1.call-update) | async-done | bytes 32784 | tf_op jit(solution)/shard_map/reduce_scatter | solution.py:125
  404.4 22.2 %reduce-scatter.3.cloned.1.call-done = f32[64,256]{1,0:T(8,128)} async-done(((f32[64,1024]{1,0:T(8,128)}), f32[64,256]{1,0:T(8,128)}) %reduce-scatter.3.cloned.1.call-update) | async-done | bytes 65552 | tf_op jit(solution)/shard_map/reduce_scatter | solution.py:124
  (142 shorter events, 55.0 us)
Async XLA Ops:
  7.2 397.3 %reduce-scatter.5.cloned.1.call-start = ((), (), s32[]{:S(2)}) async-start(), calls=%async_computation.3 | async-start | bytes 294912 | tf_op jit(solution)/shard_map/reduce_scatter | solution.py:125
  153.9 6.6 %copy-start.1 = (f32[1024]{0:T(1024)S(1)}, f32[1024]{0:T(1024)}, u32[]{:S(2)}) copy-start(f32[1024]{0:T(1024)} %param.24) | copy-start | bytes 12292
  153.9 26.5 %copy-start.2 = (f32[1024]{0:T(1024)S(1)}, f32[1024]{0:T(1024)}, u32[]{:S(2)}) copy-start(f32[1024]{0:T(1024)} %param.25) | copy-start | bytes 12292
  342.9 1.4 copy-start
  345.4 81.2 %reduce-scatter.3.cloned.1.call-start = ((), (), s32[]{:S(2)}) async-start(), calls=%async_computation.2 | async-start | bytes 327680 | tf_op jit(solution)/shard_map/reduce_scatter | solution.py:124
Sparse Core Ops, SparseCore 0:
  345.6 58.8 reduce-scatter.4
  407.5 19.1 reduce-scatter.2
